TPU v7x, 256 devices: a whole 4x4x8 slice. The times are simulated.
256 devices in a mesh: req: 16 (over x, y), seq: 16 (over z, core).
Axes of the slice: x: 4, y: 4, z: 8, core: 2. Of those that a mesh axis runs over, the one named last changes fastest.
Arguments:
- store: bfloat16 [144, 16, 56, 1024], P('req', 'seq'), may hold values from -6 to 6
- passage_owner: int32 [16, 256, 1], P(None, 'seq'), may hold values from 0 to 15; in each aligned block of 16 rows (0 to 15, 16 to 31, ..., all dimensions but the last counted through in order) at most 2 rows name the same one
- passage_slot: int32 [16, 256], P(None, 'seq'), may hold values from 0 to 8
- sel_pos: int32 [16, 1792], P('req'), may hold values from 0 to 14335, as said below
- queries: bfloat16 [16, 1792, 2048], P('req', 'seq'), may hold values from -512 to 512
- new_kv: bfloat16 [16, 1792, 1024], P('req', 'seq'), may hold values from -6 to 6
Outputs:
- blended_kv: bfloat16 [16, 14336, 1024], P('req', 'seq')
- deviation: float32 [16, 1792, 4], P('req', 'seq')
- attended: bfloat16 [16, 1792, 2048], P('req', 'seq')
Inputs may be any that keep to these rules, and one draw needn't show every extreme that they name: `passage_owner`: within the 16 pieces of one request's position block no owner is named more than 2 times, and some block names one owner exactly 2 times. `sel_pos`: entries b * 112 to (b + 1) * 112 - 1 of a request are distinct positions of block b, between b * 896 and (b + 1) * 896 - 1.
All inputs are finite; a program needn't handle non-finite values.
Results may differ from a plain program's by a relative error of at most 0.005.
Values may be sent and summed in bfloat16 or wider, within the bound.
A program may use at most 128 MiB of HBM per device.

v0:
```python
import jax
import jax.numpy as jnp
from jax import lax
from jax.sharding import PartitionSpec as P

HEAD_DIM = 128
KV_HEADS = 4
PASSAGE = 56
PASSAGES_DEV = 16
TOK_DEV = 896
SEL_DEV = 112
Q_WIDTH = 2048
KV_WIDTH = 1024
GROUP = 4


def update(carry_state, query_rows, query_pos, key_rows, value_rows, key_pos):
    running_max, weight_sum, summed = carry_state
    row_count = query_rows.shape[0]
    score_scale = HEAD_DIM ** (-0.5)
    query_split = query_rows.reshape(row_count, KV_HEADS, GROUP, HEAD_DIM)
    scores = (
        jnp.einsum("qkgd,pkd->qkgp", query_split, key_rows, preferred_element_type=jnp.float32)
        * score_scale
    )
    visible = key_pos[None, None, None, :] <= query_pos[:, None, None, None]
    scores = jnp.where(visible, scores, -1e30)
    new_max = jnp.maximum(running_max, jnp.max(scores, axis=-1))
    weights = jnp.where(visible, jnp.exp(scores - new_max[..., None]), 0.0)
    rescale = jnp.exp(running_max - new_max)
    weight_sum = weight_sum * rescale + jnp.sum(weights, axis=-1)
    product = jnp.einsum(
        "qkgp,pkd->qkgd",
        weights.astype(jnp.bfloat16),
        value_rows,
        preferred_element_type=jnp.float32,
    )
    summed = summed * rescale[..., None] + product
    return (new_max, weight_sum, summed)


def fold_attention(groups, blended):
    initial = []
    for query_rows, query_pos in groups:
        row_count = query_rows.shape[0]
        initial.append(
            (
                jnp.full((row_count, KV_HEADS, GROUP), -1e30, jnp.float32),
                jnp.zeros((row_count, KV_HEADS, GROUP), jnp.float32),
                jnp.zeros((row_count, KV_HEADS, GROUP, HEAD_DIM), jnp.float32),
            )
        )
    carry_all = tuple(initial)
    piece = lax.all_gather(blended, "seq", axis=0, tiled=True)
    absorb_row_count = piece.shape[0]
    block_rows = 512

    def take_block(state_all, step_index):
        key_part = lax.dynamic_slice_in_dim(piece, step_index * block_rows, block_rows, 0)
        first_pos = step_index * block_rows
        key_rows = key_part[:, : KV_HEADS * HEAD_DIM].reshape(block_rows, KV_HEADS, HEAD_DIM)
        value_rows = key_part[:, KV_HEADS * HEAD_DIM :].reshape(block_rows, KV_HEADS, HEAD_DIM)
        key_pos = first_pos + jnp.arange(block_rows, dtype=jnp.int32)
        updated = []
        for (query_rows, query_pos), carry_state in zip(groups, state_all):
            updated.append(
                lax.cond(
                    first_pos <= jnp.max(query_pos),
                    lambda state_in: update(
                        state_in, query_rows, query_pos, key_rows, value_rows, key_pos
                    ),
                    lambda state_in: state_in,
                    carry_state,
                )
            )
        return (tuple(updated), None)

    carry_all, _ = lax.scan(take_block, carry_all, jnp.arange(absorb_row_count // block_rows))
    finished = []
    for (query_rows, query_pos), carry_state in zip(groups, carry_all):
        row_count = query_rows.shape[0]
        output_rows = carry_state[2] / carry_state[1][..., None]
        finished.append(output_rows.reshape(row_count, Q_WIDTH).astype(jnp.bfloat16))
    return finished


def body(store, passage_owner, passage_slot, sel_pos, queries, new_kv):
    req_index = lax.axis_index("req")
    seq_index = lax.axis_index("seq")
    owner_table = passage_owner[:, :, 0]
    my_owner = lax.dynamic_index_in_dim(owner_table, req_index, 0, keepdims=False)
    store_shard = store[:, 0]
    req_count = owner_table.shape[0]
    owner_cap = max(2, (2 * PASSAGES_DEV + req_count - 1) // req_count)
    earlier = jnp.arange(PASSAGES_DEV)[:, None] > jnp.arange(PASSAGES_DEV)[None, :]
    same_owner = owner_table[:, :, None] == owner_table[:, None, :]
    rank_table = jnp.sum(same_owner & earlier[None], axis=2)
    slot_hit = (owner_table == req_index)[:, :, None] & (
        rank_table[:, :, None] == jnp.arange(owner_cap)[None, None, :]
    )
    send_slot = jnp.sum(jnp.where(slot_hit, passage_slot[:, :, None], 0), axis=1)
    outgoing = jnp.take(store_shard, send_slot.reshape(-1), axis=0)
    outgoing = outgoing.reshape(req_count, owner_cap, PASSAGE, KV_WIDTH)
    incoming = lax.all_to_all(outgoing, "req", split_axis=0, concat_axis=0, tiled=True)
    my_rank = lax.dynamic_index_in_dim(rank_table, req_index, 0, keepdims=False)
    flat_slot = my_owner * owner_cap + my_rank
    cached = jnp.take(incoming.reshape(req_count * owner_cap, PASSAGE, KV_WIDTH), flat_slot, axis=0)
    cached = cached.reshape(TOK_DEV, KV_WIDTH)
    all_pos = sel_pos[0]
    own_pos = lax.dynamic_slice_in_dim(all_pos, seq_index * SEL_DEV, SEL_DEV)
    offset = own_pos - seq_index * TOK_DEV
    fresh_rows = new_kv[0]
    picked = jnp.take(cached, offset, axis=0)
    blended = cached.at[offset].set(fresh_rows)
    difference = fresh_rows.astype(jnp.float32) - picked.astype(jnp.float32)
    squared = (difference * difference).reshape(SEL_DEV, 2, KV_HEADS, HEAD_DIM)
    deviation = jnp.sum(squared, axis=(1, 3))
    query_local = queries[0]
    attended = fold_attention([(query_local, own_pos)], blended)[0]
    return (blended[None], deviation[None], attended[None])


def solution(mesh):
    placed = (
        P("req", "seq", None, None),
        P(None, "seq", None),
        P(None, "seq"),
        P("req", None),
        P("req", "seq", None),
        P("req", "seq", None),
    )
    return jax.shard_map(
        body,
        mesh=mesh,
        in_specs=placed,
        out_specs=(P("req", "seq", None), P("req", "seq", None), P("req", "seq", None)),
        check_vma=False,
    )
```

profile of v0, /device:TPU:225, one launch (start us, length us, event | category | flops | bytes accessed | tf_op | source)
XLA Modules:
  0.0 505.5 jit_solution(7057776193855823319)
XLA Ops:
  17.2 6.8 %all-to-all-start = ((bf16[16,2,56,1024]{3,2,1,0:T(8,128)(2,1)}), bf16[16,2,56,1024]{3,2,1,0:T(8,128)(2,1)}, u32[]{:S(2)}, u32[]{:S(2)}) async-start(bf16[16,2,56,1024]{3,2,1,0:T(8,128)(2,1)} %broadcast_select_fusion), calls=%async_computation | async-start | bytes 7340032 | tf_op jit(solution)/shard_map/all_to_all | solution.py:104
  27.0 45.7 %all-to-all-done = bf16[16,2,56,1024]{3,2,1,0:T(8,128)(2,1)} async-done(((bf16[16,2,56,1024]{3,2,1,0:T(8,128)(2,1)}), bf16[16,2,56,1024]{3,2,1,0:T(8,128)(2,1)}, u32[]{:S(2)}, u32[]{:S(2)}) %all-to-all-start) | async-done | bytes 3670048 | tf_op jit(solution)/shard_map/all_to_all | solution.py:104
  84.1 158.5 %all-gather.2.cloned.1.call-done = bf16[14336,1024]{1,0:T(8,128)(2,1)} async-done(((bf16[896,1024]{1,0:T(8,128)(2,1)}), bf16[14336,1024]{1,0:T(8,128)(2,1)}) %all-gather.2.cloned.1.call-update) | async-done | bytes 29360144 | tf_op jit(solution)/shard_map/all_gather | solution.py:54
  242.6 35.1 %copy.27 = bf16[14336,1024]{0,1:T(8,128)(2,1)} copy(bf16[14336,1024]{1,0:T(8,128)(2,1)} %all-gather.2.cloned.1.call-done) | data formatting | bytes 58720256 | tf_op jit(solution)/shard_map/while | solution.py:78
  277.8 219.3 %while.15 = (s32[]{:T(128)}, f32[112,4,4]{0,2,1:T(4,128)S(1)}, f32[112,4,4]{0,2,1:T(4,128)S(1)}, f32[112,4,4,128]{3,0,2,1:T(8,128)S(1)}, s32[28]{0:T(128)S(1)}, ...) while((s32[]{:T(128)}, f32[112,4,4]{0,2,1:T(4,128)S(1)}, ...), condition=%wide.region_10.11_spmd, body=%wide.region_5.10_spmd.sunk | while | flops 482209792 | bytes 17720068 | solution.py:78
  279.7 5.9 %conditional.2 = ((f32[112,4,4]{0,2,1:T(4,128)S(1)}, f32[112,4,4]{0,2,1:T(4,128)S(1)}, f32[112,4,4,128]{3,0,2,1:T(8,128)S(1)})) conditional(s32[]{:T(128)} %convert_element_type.61, (f32[112,4,4]{0,2,1:T(4,128)S(1)}, f32[112,4,4]{0,2,1:T(4,128)S(1)}, f32[112,4,4,128]{3,0,2,1:T(8,128)S(1)}) %tuple.51, (s32[]{:T(128)}, s32[512]{0:T(512)S(1)}, ...), branch_computations={%region_6.6_spmd, %region_7.9_spmd} | conditional | flops 482209792 | bytes 17717786 | solution.py:67
  287.5 5.9 %conditional.2 = ((f32[112,4,4]{0,2,1:T(4,128)S(1)}, f32[112,4,4]{0,2,1:T(4,128)S(1)}, f32[112,4,4,128]{3,0,2,1:T(8,128)S(1)})) conditional(s32[]{:T(128)} %convert_element_type.61, (f32[112,4,4]{0,2,1:T(4,128)S(1)}, f32[112,4,4]{0,2,1:T(4,128)S(1)}, f32[112,4,4,128]{3,0,2,1:T(8,128)S(1)}) %tuple.51, (s32[]{:T(128)}, s32[512]{0:T(512)S(1)}, ...), branch_computations={%region_6.6_spmd, %region_7.9_spmd} | conditional | flops 482209792 | bytes 17717786 | solution.py:67
  295.4 5.9 %conditional.2 = ((f32[112,4,4]{0,2,1:T(4,128)S(1)}, f32[112,4,4]{0,2,1:T(4,128)S(1)}, f32[112,4,4,128]{3,0,2,1:T(8,128)S(1)})) conditional(s32[]{:T(128)} %convert_element_type.61, (f32[112,4,4]{0,2,1:T(4,128)S(1)}, f32[112,4,4]{0,2,1:T(4,128)S(1)}, f32[112,4,4,128]{3,0,2,1:T(8,128)S(1)}) %tuple.51, (s32[]{:T(128)}, s32[512]{0:T(512)S(1)}, ...), branch_computations={%region_6.6_spmd, %region_7.9_spmd} | conditional | flops 482209792 | bytes 17717786 | solution.py:67
  303.2 5.9 %conditional.2 = ((f32[112,4,4]{0,2,1:T(4,128)S(1)}, f32[112,4,4]{0,2,1:T(4,128)S(1)}, f32[112,4,4,128]{3,0,2,1:T(8,128)S(1)})) conditional(s32[]{:T(128)} %convert_element_type.61, (f32[112,4,4]{0,2,1:T(4,128)S(1)}, f32[112,4,4]{0,2,1:T(4,128)S(1)}, f32[112,4,4,128]{3,0,2,1:T(8,128)S(1)}) %tuple.51, (s32[]{:T(128)}, s32[512]{0:T(512)S(1)}, ...), branch_computations={%region_6.6_spmd, %region_7.9_spmd} | conditional | flops 482209792 | bytes 17717786 | solution.py:67
  311.0 5.9 %conditional.2 = ((f32[112,4,4]{0,2,1:T(4,128)S(1)}, f32[112,4,4]{0,2,1:T(4,128)S(1)}, f32[112,4,4,128]{3,0,2,1:T(8,128)S(1)})) conditional(s32[]{:T(128)} %convert_element_type.61, (f32[112,4,4]{0,2,1:T(4,128)S(1)}, f32[112,4,4]{0,2,1:T(4,128)S(1)}, f32[112,4,4,128]{3,0,2,1:T(8,128)S(1)}) %tuple.51, (s32[]{:T(128)}, s32[512]{0:T(512)S(1)}, ...), branch_computations={%region_6.6_spmd, %region_7.9_spmd} | conditional | flops 482209792 | bytes 17717786 | solution.py:67
  318.9 5.9 %conditional.2 = ((f32[112,4,4]{0,2,1:T(4,128)S(1)}, f32[112,4,4]{0,2,1:T(4,128)S(1)}, f32[112,4,4,128]{3,0,2,1:T(8,128)S(1)})) conditional(s32[]{:T(128)} %convert_element_type.61, (f32[112,4,4]{0,2,1:T(4,128)S(1)}, f32[112,4,4]{0,2,1:T(4,128)S(1)}, f32[112,4,4,128]{3,0,2,1:T(8,128)S(1)}) %tuple.51, (s32[]{:T(128)}, s32[512]{0:T(512)S(1)}, ...), branch_computations={%region_6.6_spmd, %region_7.9_spmd} | conditional | flops 482209792 | bytes 17717786 | solution.py:67
  326.7 5.9 %conditional.2 = ((f32[112,4,4]{0,2,1:T(4,128)S(1)}, f32[112,4,4]{0,2,1:T(4,128)S(1)}, f32[112,4,4,128]{3,0,2,1:T(8,128)S(1)})) conditional(s32[]{:T(128)} %convert_element_type.61, (f32[112,4,4]{0,2,1:T(4,128)S(1)}, f32[112,4,4]{0,2,1:T(4,128)S(1)}, f32[112,4,4,128]{3,0,2,1:T(8,128)S(1)}) %tuple.51, (s32[]{:T(128)}, s32[512]{0:T(512)S(1)}, ...), branch_computations={%region_6.6_spmd, %region_7.9_spmd} | conditional | flops 482209792 | bytes 17717786 | solution.py:67
  334.5 5.9 %conditional.2 = ((f32[112,4,4]{0,2,1:T(4,128)S(1)}, f32[112,4,4]{0,2,1:T(4,128)S(1)}, f32[112,4,4,128]{3,0,2,1:T(8,128)S(1)})) conditional(s32[]{:T(128)} %convert_element_type.61, (f32[112,4,4]{0,2,1:T(4,128)S(1)}, f32[112,4,4]{0,2,1:T(4,128)S(1)}, f32[112,4,4,128]{3,0,2,1:T(8,128)S(1)}) %tuple.51, (s32[]{:T(128)}, s32[512]{0:T(512)S(1)}, ...), branch_computations={%region_6.6_spmd, %region_7.9_spmd} | conditional | flops 482209792 | bytes 17717786 | solution.py:67
  342.4 5.9 %conditional.2 = ((f32[112,4,4]{0,2,1:T(4,128)S(1)}, f32[112,4,4]{0,2,1:T(4,128)S(1)}, f32[112,4,4,128]{3,0,2,1:T(8,128)S(1)})) conditional(s32[]{:T(128)} %convert_element_type.61, (f32[112,4,4]{0,2,1:T(4,128)S(1)}, f32[112,4,4]{0,2,1:T(4,128)S(1)}, f32[112,4,4,128]{3,0,2,1:T(8,128)S(1)}) %tuple.51, (s32[]{:T(128)}, s32[512]{0:T(512)S(1)}, ...), branch_computations={%region_6.6_spmd, %region_7.9_spmd} | conditional | flops 482209792 | bytes 17717786 | solution.py:67
  350.2 5.9 %conditional.2 = ((f32[112,4,4]{0,2,1:T(4,128)S(1)}, f32[112,4,4]{0,2,1:T(4,128)S(1)}, f32[112,4,4,128]{3,0,2,1:T(8,128)S(1)})) conditional(s32[]{:T(128)} %convert_element_type.61, (f32[112,4,4]{0,2,1:T(4,128)S(1)}, f32[112,4,4]{0,2,1:T(4,128)S(1)}, f32[112,4,4,128]{3,0,2,1:T(8,128)S(1)}) %tuple.51, (s32[]{:T(128)}, s32[512]{0:T(512)S(1)}, ...), branch_computations={%region_6.6_spmd, %region_7.9_spmd} | conditional | flops 482209792 | bytes 17717786 | solution.py:67
  358.0 5.9 %conditional.2 = ((f32[112,4,4]{0,2,1:T(4,128)S(1)}, f32[112,4,4]{0,2,1:T(4,128)S(1)}, f32[112,4,4,128]{3,0,2,1:T(8,128)S(1)})) conditional(s32[]{:T(128)} %convert_element_type.61, (f32[112,4,4]{0,2,1:T(4,128)S(1)}, f32[112,4,4]{0,2,1:T(4,128)S(1)}, f32[112,4,4,128]{3,0,2,1:T(8,128)S(1)}) %tuple.51, (s32[]{:T(128)}, s32[512]{0:T(512)S(1)}, ...), branch_computations={%region_6.6_spmd, %region_7.9_spmd} | conditional | flops 482209792 | bytes 17717786 | solution.py:67
  365.9 5.9 %conditional.2 = ((f32[112,4,4]{0,2,1:T(4,128)S(1)}, f32[112,4,4]{0,2,1:T(4,128)S(1)}, f32[112,4,4,128]{3,0,2,1:T(8,128)S(1)})) conditional(s32[]{:T(128)} %convert_element_type.61, (f32[112,4,4]{0,2,1:T(4,128)S(1)}, f32[112,4,4]{0,2,1:T(4,128)S(1)}, f32[112,4,4,128]{3,0,2,1:T(8,128)S(1)}) %tuple.51, (s32[]{:T(128)}, s32[512]{0:T(512)S(1)}, ...), branch_computations={%region_6.6_spmd, %region_7.9_spmd} | conditional | flops 482209792 | bytes 17717786 | solution.py:67
  373.7 5.9 %conditional.2 = ((f32[112,4,4]{0,2,1:T(4,128)S(1)}, f32[112,4,4]{0,2,1:T(4,128)S(1)}, f32[112,4,4,128]{3,0,2,1:T(8,128)S(1)})) conditional(s32[]{:T(128)} %convert_element_type.61, (f32[112,4,4]{0,2,1:T(4,128)S(1)}, f32[112,4,4]{0,2,1:T(4,128)S(1)}, f32[112,4,4,128]{3,0,2,1:T(8,128)S(1)}) %tuple.51, (s32[]{:T(128)}, s32[512]{0:T(512)S(1)}, ...), branch_computations={%region_6.6_spmd, %region_7.9_spmd} | conditional | flops 482209792 | bytes 17717786 | solution.py:67
  381.5 5.9 %conditional.2 = ((f32[112,4,4]{0,2,1:T(4,128)S(1)}, f32[112,4,4]{0,2,1:T(4,128)S(1)}, f32[112,4,4,128]{3,0,2,1:T(8,128)S(1)})) conditional(s32[]{:T(128)} %convert_element_type.61, (f32[112,4,4]{0,2,1:T(4,128)S(1)}, f32[112,4,4]{0,2,1:T(4,128)S(1)}, f32[112,4,4,128]{3,0,2,1:T(8,128)S(1)}) %tuple.51, (s32[]{:T(128)}, s32[512]{0:T(512)S(1)}, ...), branch_computations={%region_6.6_spmd, %region_7.9_spmd} | conditional | flops 482209792 | bytes 17717786 | solution.py:67
  389.4 5.9 %conditional.2 = ((f32[112,4,4]{0,2,1:T(4,128)S(1)}, f32[112,4,4]{0,2,1:T(4,128)S(1)}, f32[112,4,4,128]{3,0,2,1:T(8,128)S(1)})) conditional(s32[]{:T(128)} %convert_element_type.61, (f32[112,4,4]{0,2,1:T(4,128)S(1)}, f32[112,4,4]{0,2,1:T(4,128)S(1)}, f32[112,4,4,128]{3,0,2,1:T(8,128)S(1)}) %tuple.51, (s32[]{:T(128)}, s32[512]{0:T(512)S(1)}, ...), branch_computations={%region_6.6_spmd, %region_7.9_spmd} | conditional | flops 482209792 | bytes 17717786 | solution.py:67
  397.2 5.9 %conditional.2 = ((f32[112,4,4]{0,2,1:T(4,128)S(1)}, f32[112,4,4]{0,2,1:T(4,128)S(1)}, f32[112,4,4,128]{3,0,2,1:T(8,128)S(1)})) conditional(s32[]{:T(128)} %convert_element_type.61, (f32[112,4,4]{0,2,1:T(4,128)S(1)}, f32[112,4,4]{0,2,1:T(4,128)S(1)}, f32[112,4,4,128]{3,0,2,1:T(8,128)S(1)}) %tuple.51, (s32[]{:T(128)}, s32[512]{0:T(512)S(1)}, ...), branch_computations={%region_6.6_spmd, %region_7.9_spmd} | conditional | flops 482209792 | bytes 17717786 | solution.py:67
  405.0 5.9 %conditional.2 = ((f32[112,4,4]{0,2,1:T(4,128)S(1)}, f32[112,4,4]{0,2,1:T(4,128)S(1)}, f32[112,4,4,128]{3,0,2,1:T(8,128)S(1)})) conditional(s32[]{:T(128)} %convert_element_type.61, (f32[112,4,4]{0,2,1:T(4,128)S(1)}, f32[112,4,4]{0,2,1:T(4,128)S(1)}, f32[112,4,4,128]{3,0,2,1:T(8,128)S(1)}) %tuple.51, (s32[]{:T(128)}, s32[512]{0:T(512)S(1)}, ...), branch_computations={%region_6.6_spmd, %region_7.9_spmd} | conditional | flops 482209792 | bytes 17717786 | solution.py:67
  412.9 5.9 %conditional.2 = ((f32[112,4,4]{0,2,1:T(4,128)S(1)}, f32[112,4,4]{0,2,1:T(4,128)S(1)}, f32[112,4,4,128]{3,0,2,1:T(8,128)S(1)})) conditional(s32[]{:T(128)} %convert_element_type.61, (f32[112,4,4]{0,2,1:T(4,128)S(1)}, f32[112,4,4]{0,2,1:T(4,128)S(1)}, f32[112,4,4,128]{3,0,2,1:T(8,128)S(1)}) %tuple.51, (s32[]{:T(128)}, s32[512]{0:T(512)S(1)}, ...), branch_computations={%region_6.6_spmd, %region_7.9_spmd} | conditional | flops 482209792 | bytes 17717786 | solution.py:67
  420.7 5.9 %conditional.2 = ((f32[112,4,4]{0,2,1:T(4,128)S(1)}, f32[112,4,4]{0,2,1:T(4,128)S(1)}, f32[112,4,4,128]{3,0,2,1:T(8,128)S(1)})) conditional(s32[]{:T(128)} %convert_element_type.61, (f32[112,4,4]{0,2,1:T(4,128)S(1)}, f32[112,4,4]{0,2,1:T(4,128)S(1)}, f32[112,4,4,128]{3,0,2,1:T(8,128)S(1)}) %tuple.51, (s32[]{:T(128)}, s32[512]{0:T(512)S(1)}, ...), branch_computations={%region_6.6_spmd, %region_7.9_spmd} | conditional | flops 482209792 | bytes 17717786 | solution.py:67
  428.5 5.9 %conditional.2 = ((f32[112,4,4]{0,2,1:T(4,128)S(1)}, f32[112,4,4]{0,2,1:T(4,128)S(1)}, f32[112,4,4,128]{3,0,2,1:T(8,128)S(1)})) conditional(s32[]{:T(128)} %convert_element_type.61, (f32[112,4,4]{0,2,1:T(4,128)S(1)}, f32[112,4,4]{0,2,1:T(4,128)S(1)}, f32[112,4,4,128]{3,0,2,1:T(8,128)S(1)}) %tuple.51, (s32[]{:T(128)}, s32[512]{0:T(512)S(1)}, ...), branch_computations={%region_6.6_spmd, %region_7.9_spmd} | conditional | flops 482209792 | bytes 17717786 | solution.py:67
  436.4 5.9 %conditional.2 = ((f32[112,4,4]{0,2,1:T(4,128)S(1)}, f32[112,4,4]{0,2,1:T(4,128)S(1)}, f32[112,4,4,128]{3,0,2,1:T(8,128)S(1)})) conditional(s32[]{:T(128)} %convert_element_type.61, (f32[112,4,4]{0,2,1:T(4,128)S(1)}, f32[112,4,4]{0,2,1:T(4,128)S(1)}, f32[112,4,4,128]{3,0,2,1:T(8,128)S(1)}) %tuple.51, (s32[]{:T(128)}, s32[512]{0:T(512)S(1)}, ...), branch_computations={%region_6.6_spmd, %region_7.9_spmd} | conditional | flops 482209792 | bytes 17717786 | solution.py:67
  444.2 5.9 %conditional.2 = ((f32[112,4,4]{0,2,1:T(4,128)S(1)}, f32[112,4,4]{0,2,1:T(4,128)S(1)}, f32[112,4,4,128]{3,0,2,1:T(8,128)S(1)})) conditional(s32[]{:T(128)} %convert_element_type.61, (f32[112,4,4]{0,2,1:T(4,128)S(1)}, f32[112,4,4]{0,2,1:T(4,128)S(1)}, f32[112,4,4,128]{3,0,2,1:T(8,128)S(1)}) %tuple.51, (s32[]{:T(128)}, s32[512]{0:T(512)S(1)}, ...), branch_computations={%region_6.6_spmd, %region_7.9_spmd} | conditional | flops 482209792 | bytes 17717786 | solution.py:67
  452.0 5.9 %conditional.2 = ((f32[112,4,4]{0,2,1:T(4,128)S(1)}, f32[112,4,4]{0,2,1:T(4,128)S(1)}, f32[112,4,4,128]{3,0,2,1:T(8,128)S(1)})) conditional(s32[]{:T(128)} %convert_element_type.61, (f32[112,4,4]{0,2,1:T(4,128)S(1)}, f32[112,4,4]{0,2,1:T(4,128)S(1)}, f32[112,4,4,128]{3,0,2,1:T(8,128)S(1)}) %tuple.51, (s32[]{:T(128)}, s32[512]{0:T(512)S(1)}, ...), branch_computations={%region_6.6_spmd, %region_7.9_spmd} | conditional | flops 482209792 | bytes 17717786 | solution.py:67
  459.9 5.9 %conditional.2 = ((f32[112,4,4]{0,2,1:T(4,128)S(1)}, f32[112,4,4]{0,2,1:T(4,128)S(1)}, f32[112,4,4,128]{3,0,2,1:T(8,128)S(1)})) conditional(s32[]{:T(128)} %convert_element_type.61, (f32[112,4,4]{0,2,1:T(4,128)S(1)}, f32[112,4,4]{0,2,1:T(4,128)S(1)}, f32[112,4,4,128]{3,0,2,1:T(8,128)S(1)}) %tuple.51, (s32[]{:T(128)}, s32[512]{0:T(512)S(1)}, ...), branch_computations={%region_6.6_spmd, %region_7.9_spmd} | conditional | flops 482209792 | bytes 17717786 | solution.py:67
  467.7 5.9 %conditional.2 = ((f32[112,4,4]{0,2,1:T(4,128)S(1)}, f32[112,4,4]{0,2,1:T(4,128)S(1)}, f32[112,4,4,128]{3,0,2,1:T(8,128)S(1)})) conditional(s32[]{:T(128)} %convert_element_type.61, (f32[112,4,4]{0,2,1:T(4,128)S(1)}, f32[112,4,4]{0,2,1:T(4,128)S(1)}, f32[112,4,4,128]{3,0,2,1:T(8,128)S(1)}) %tuple.51, (s32[]{:T(128)}, s32[512]{0:T(512)S(1)}, ...), branch_computations={%region_6.6_spmd, %region_7.9_spmd} | conditional | flops 482209792 | bytes 17717786 | solution.py:67
  475.5 5.9 %conditional.2 = ((f32[112,4,4]{0,2,1:T(4,128)S(1)}, f32[112,4,4]{0,2,1:T(4,128)S(1)}, f32[112,4,4,128]{3,0,2,1:T(8,128)S(1)})) conditional(s32[]{:T(128)} %convert_element_type.61, (f32[112,4,4]{0,2,1:T(4,128)S(1)}, f32[112,4,4]{0,2,1:T(4,128)S(1)}, f32[112,4,4,128]{3,0,2,1:T(8,128)S(1)}) %tuple.51, (s32[]{:T(128)}, s32[512]{0:T(512)S(1)}, ...), branch_computations={%region_6.6_spmd, %region_7.9_spmd} | conditional | flops 482209792 | bytes 17717786 | solution.py:67
  483.4 5.9 %conditional.2 = ((f32[112,4,4]{0,2,1:T(4,128)S(1)}, f32[112,4,4]{0,2,1:T(4,128)S(1)}, f32[112,4,4,128]{3,0,2,1:T(8,128)S(1)})) conditional(s32[]{:T(128)} %convert_element_type.61, (f32[112,4,4]{0,2,1:T(4,128)S(1)}, f32[112,4,4]{0,2,1:T(4,128)S(1)}, f32[112,4,4,128]{3,0,2,1:T(8,128)S(1)}) %tuple.51, (s32[]{:T(128)}, s32[512]{0:T(512)S(1)}, ...), branch_computations={%region_6.6_spmd, %region_7.9_spmd} | conditional | flops 482209792 | bytes 17717786 | solution.py:67
  (386 shorter events, 212.5 us)
Async XLA Ops:
  7.2 3.2 copy-start
  17.2 55.5 %all-to-all-start = ((bf16[16,2,56,1024]{3,2,1,0:T(8,128)(2,1)}), bf16[16,2,56,1024]{3,2,1,0:T(8,128)(2,1)}, u32[]{:S(2)}, u32[]{:S(2)}) async-start(bf16[16,2,56,1024]{3,2,1,0:T(8,128)(2,1)} %broadcast_select_fusion), calls=%async_computation | async-start | bytes 7340032 | tf_op jit(solution)/shard_map/all_to_all | solution.py:104
  76.6 2.7 copy-start.4
  79.2 163.4 %all-gather.2.cloned.1.call-start = ((), (), s32[]{:S(2)}) async-start(), calls=%async_computation.1 | async-start | bytes 31195136 | tf_op jit(solution)/shard_map/all_gather | solution.py:54
  81.4 1.2 copy-start.2
  84.1 193.7 %copy-start.3 = (bf16[1,112,2048]{2,1,0:T(8,128)(2,1)S(1)}, bf16[1,112,2048]{2,1,0:T(8,128)(2,1)}, u32[]{:S(2)}) copy-start(bf16[1,112,2048]{2,1,0:T(8,128)(2,1)} %param.14) | copy-start | bytes 1376260
  497.0 1.6 copy-start.1
Sparse Core Ops, SparseCore 0:
  82.8 159.7 all-gather.1
where the time goes:
time: 508 us; the launch traced here: 506 us
  waiting for transfers between devices  204 us (40%)
  local copies, waits for them, and re-layouts  127 us (25%)
  matrix products  65.1 us (13%)
  other arithmetic  49.5 us (10%)
  loops' own time  38.6 us (8%)
  between operations  14.2 us (3%)
  starting transfers between devices  6.84 us (1%)
    all_gather x1, waiting for transfers between devices, fold_attention(): piece = lax.all_gather(blended, 'seq', axis=0, tiled=True)  159 us
    slice x28, local copies, waits for them, and re-layouts, take_block(): key_part[:, KV_HEADS * HEAD_DIM:].reshape(block_rows, KV_HEADS, HEAD_DIM)  52.1 us
    all_to_all x1, waiting for transfers between devices, body(): lax.all_to_all(outgoing, 'req', split_axis=0, concat_axis=0, tiled=True)  45.7 us
    dot_general x28, matrix products, update(): jnp.einsum('qkgp,pkd->qkgd', weights.astype(jnp.bfloat16), value_rows, pr...  42.1 us
    another operation x1, loops' own time, fold_attention(): lax.scan(take_block, carry_all, jnp.arange(absorb_row_count // block_rows))  36.9 us
    while x1, local copies, waits for them, and re-layouts, fold_attention(): lax.scan(take_block, carry_all, jnp.arange(absorb_row_count // block_rows))  35.1 us
    reduce_sum x28, other arithmetic, update(): weight_sum = weight_sum * rescale + jnp.sum(weights, axis=-1)  33.8 us
    dot_general x28, matrix products, update(): jnp.einsum('qkgd,pkd->qkgp', query_split, key_rows, preferred_element_typ...  23.1 us
  transfers between devices with their start and end apart: 2, of which 2 were waited for; matrix products, arithmetic and copies ran while one was open for 1% of the time, Pallas kernels for 0%

commit v1 on v0

--- a/solution.py
+++ b/solution.py
@@ -51,7 +51,9 @@
             )
         )
     carry_all = tuple(initial)
-    piece = lax.all_gather(blended, "seq", axis=0, tiled=True)
+    piece = jnp.concatenate(
+        lax.all_to_all(jnp.stack([blended] * lax.axis_size("seq")), "seq", 0, 0), axis=0
+    )
     absorb_row_count = piece.shape[0]
     block_rows = 512
 

time: 508 us -> 1030 us (2.03)
  waiting for transfers between devices: 204 us -> 677 us
  local copies, waits for them, and re-layouts: 127 us -> 180 us
  between operations: 14.2 us -> 0.83 us
    all_to_all x0 -> x1, waiting for transfers between devices: none -> 631 us  [fold_attention(): lax.all_to_all(jnp.stack([blended] * lax.axis_size('seq')), 'seq', 0, 0)]
    all_gather x1 -> x0, waiting for transfers between devices: 159 us -> none  [fold_attention(): piece = lax.all_gather(blended, 'seq', axis=0, tiled=True)]
    all_to_all x0 -> x1, local copies, waits for them, and re-layouts: none -> 41 us  [fold_attention(): lax.all_to_all(jnp.stack([blended] * lax.axis_size('seq')), 'seq', 0, 0)]
    another operation x0 -> x1, local copies, waits for them, and re-layouts: none -> 11.1 us  [fold_attention(): jnp.stack([blended] * lax.axis_size('seq'))]
  transfers between devices with their start and end apart: 2 -> 2, of which waited for: 2 -> 2; matrix products, arithmetic and copies ran while one was open for 1% -> 0% of each run, Pallas kernels for 0% -> 0%
where the time goes in v1:
time: 1030 us
  waiting for transfers between devices  677 us (66%)
  local copies, waits for them, and re-layouts  180 us (17%)
  matrix products  65.1 us (6%)
  other arithmetic  49.5 us (5%)
  loops' own time  38.6 us (4%)
  starting transfers between devices  14.1 us (1%)
    all_to_all x1, waiting for transfers between devices, fold_attention(): lax.all_to_all(jnp.stack([blended] * lax.axis_size('seq')), 'seq', 0, 0)  631 us
    slice x28, local copies, waits for them, and re-layouts, take_block(): key_part[:, KV_HEADS * HEAD_DIM:].reshape(block_rows, KV_HEADS, HEAD_DIM)  52.1 us
    all_to_all x1, waiting for transfers between devices, body(): lax.all_to_all(outgoing, 'req', split_axis=0, concat_axis=0, tiled=True)  45.7 us
    dot_general x28, matrix products, update(): jnp.einsum('qkgp,pkd->qkgd', weights.astype(jnp.bfloat16), value_rows, pr...  42.1 us
    all_to_all x1, local copies, waits for them, and re-layouts, fold_attention(): lax.all_to_all(jnp.stack([blended] * lax.axis_size('seq')), 'seq', 0, 0)  41 us
    another operation x1, loops' own time, fold_attention(): lax.scan(take_block, carry_all, jnp.arange(absorb_row_count // block_rows))  36.9 us
    while x1, local copies, waits for them, and re-layouts, fold_attention(): lax.scan(take_block, carry_all, jnp.arange(absorb_row_count // block_rows))  35.1 us
    reduce_sum x28, other arithmetic, update(): weight_sum = weight_sum * rescale + jnp.sum(weights, axis=-1)  33.8 us
  transfers between devices with their start and end apart: 2, of which 2 were waited for; matrix products, arithmetic and copies ran while one was open for 0% of the time, Pallas kernels for 0%

profile of v1, /device:TPU:225, one launch (start us, length us, event | category | flops | bytes accessed | tf_op | source)
XLA Modules:
  0.0 1025.2 jit_solution(7445030610221001740)
XLA Ops:
  10.7 6.8 all-to-all-start
  20.5 45.7 %all-to-all-done = bf16[16,2,56,1024]{3,2,1,0:T(8,128)(2,1)} async-done(((bf16[16,2,56,1024]{3,2,1,0:T(8,128)(2,1)}), bf16[16,2,56,1024]{3,2,1,0:T(8,128)(2,1)}, u32[]{:S(2)}, u32[]{:S(2)}) %all-to-all-start) | async-done | bytes 3670048 | tf_op jit(solution)/shard_map/all_to_all | solution.py:106
  77.4 11.1 %stack.2 = bf16[16,896,1024]{1,2,0:T(8,128)(2,1)} broadcast(bf16[896,1024]{0,1:T(8,128)(2,1)} %copy.35), dimensions={1,2} | broadcast | bytes 31195136 | tf_op jit(solution)/shard_map/stack | solution.py:55
  88.4 7.3 all-to-all-start.1
  97.2 630.9 %all-to-all-done.1 = bf16[16,896,1024]{1,2,0:T(8,128)(2,1)} async-done(((bf16[16,896,1024]{1,2,0:T(8,128)(2,1)}), bf16[16,896,1024]{1,2,0:T(8,128)(2,1)}, u32[]{:S(2)}, u32[]{:S(2)}) %all-to-all-start.1) | async-done | bytes 29360160 | tf_op jit(solution)/shard_map/all_to_all | solution.py:55
  728.1 41.0 %copy.36 = bf16[16,896,1024]{2,1,0:T(8,128)(2,1)} copy(bf16[16,896,1024]{1,2,0:T(8,128)(2,1)} %all-to-all-done.1) | data formatting | bytes 58720256 | tf_op jit(solution)/shard_map/all_to_all | solution.py:55
  769.1 35.1 %copy.37 = bf16[14336,1024]{0,1:T(8,128)(2,1)} copy(bf16[14336,1024]{1,0:T(8,128)(2,1)} %bitcast.78) | data formatting | bytes 58720256 | tf_op jit(solution)/shard_map/while | solution.py:80
  804.3 219.3 %while.15 = (s32[]{:T(128)}, f32[112,4,4]{0,2,1:T(4,128)S(1)}, f32[112,4,4]{0,2,1:T(4,128)S(1)}, f32[112,4,4,128]{3,0,2,1:T(8,128)S(1)}, s32[28]{0:T(128)S(1)}, ...) while((s32[]{:T(128)}, f32[112,4,4]{0,2,1:T(4,128)S(1)}, ...), condition=%wide.region_10.11_spmd, body=%wide.region_5.10_spmd.sunk | while | flops 482209792 | bytes 17720068 | solution.py:80
  806.3 5.9 conditional.2
  814.1 5.9 conditional.2
  821.9 5.9 conditional.2
  829.8 5.9 conditional.2
  837.6 5.9 conditional.2
  845.4 5.9 conditional.2
  853.3 5.9 conditional.2
  861.1 5.9 conditional.2
  868.9 5.9 conditional.2
  876.8 5.9 conditional.2
  884.6 5.9 conditional.2
  892.4 5.9 conditional.2
  900.3 5.9 conditional.2
  908.1 5.9 conditional.2
  915.9 5.9 conditional.2
  923.8 5.9 conditional.2
  931.6 5.9 conditional.2
  939.4 5.9 conditional.2
  947.3 5.9 conditional.2
  955.1 5.9 conditional.2
  963.0 5.9 conditional.2
  970.8 5.9 conditional.2
  994.3 5.9 conditional.2
  1002.1 5.9 conditional.2
  (388 shorter events, 231.4 us)
Async XLA Ops:
  0.6 3.2 copy-start
  10.7 55.5 %all-to-all-start = ((bf16[16,2,56,1024]{3,2,1,0:T(8,128)(2,1)}), bf16[16,2,56,1024]{3,2,1,0:T(8,128)(2,1)}, u32[]{:S(2)}, u32[]{:S(2)}) async-start(bf16[16,2,56,1024]{3,2,1,0:T(8,128)(2,1)} %broadcast_select_fusion), calls=%async_computation | async-start | bytes 7340032 | tf_op jit(solution)/shard_map/all_to_all | solution.py:106
  70.1 2.6 copy-start.4
  74.8 13.6 %copy-start.2 = (bf16[896,1024]{1,0:T(8,128)(2,1)}, bf16[896,1024]{1,0:T(8,128)(2,1)S(1)}, u32[]{:S(2)}) copy-start(bf16[896,1024]{1,0:T(8,128)(2,1)S(1)} %scatter_custom_fusion) | copy-start | bytes 5505028
  88.4 639.6 %all-to-all-start.1 = ((bf16[16,896,1024]{1,2,0:T(8,128)(2,1)}), bf16[16,896,1024]{1,2,0:T(8,128)(2,1)}, u32[]{:S(2)}, u32[]{:S(2)}) async-start(bf16[16,896,1024]{1,2,0:T(8,128)(2,1)} %stack.2), calls=%async_computation.1 | async-start | bytes 58720256 | tf_op jit(solution)/shard_map/all_to_all | solution.py:55
  769.1 35.2 %copy-start.3 = (bf16[1,112,2048]{2,1,0:T(8,128)(2,1)S(1)}, bf16[1,112,2048]{2,1,0:T(8,128)(2,1)}, u32[]{:S(2)}) copy-start(bf16[1,112,2048]{2,1,0:T(8,128)(2,1)} %param.14) | copy-start | bytes 1376260
  1023.6 1.6 copy-start.1
